TPU v7x, 32 devices: a whole 2x2x4 slice. The times are simulated.
32 devices in a mesh: freq: 8 (over z, core), tile: 4 (over y, x).
Axes of the slice: x: 2, y: 2, z: 4, core: 2. Of those that a mesh axis runs over, the one named last changes fastest.
Arguments:
- wave: float32 [2, 2, 8, 256, 1024], P(None, None, 'freq', 'tile'), may hold values from -6 to 6
- velocity: float32 [3, 256, 1024], P(None, 'tile'), may hold values from 1500 to 4500
Outputs:
- image: float32 [3, 16, 256, 1024], P(None, 'freq', 'tile')
All inputs are finite; a program needn't handle non-finite values.
Results may differ from a plain program's by a relative error of at most 0.0001.
Values sent between devices are 32-bit elements; how exact they have to be, the bound alone decides.
A program may use at most 128 MiB of HBM per device.

v0:
```python
import math

import jax
import jax.numpy as jnp
from jax import lax
from jax.sharding import PartitionSpec as P

STEPS = 3
SWEEPS = 8
OFFS = 16


pade_first = 0.376393
pade_second = 0.478242
layer_thickness = 10.0
grid_spacing = 15.0
full_turn = 2.0 * math.pi


def extended_2(cells, sides, width):
    for axis, dim in sides:
        count = lax.axis_size(axis)
        ends = count - 1
        head = lax.slice_in_dim(cells, 0, width, axis=dim)
        tail = lax.slice_in_dim(cells, cells.shape[dim] - width, cells.shape[dim], axis=dim)
        cells = jnp.concatenate(
            [
                lax.ppermute(tail, axis, [(i, (i + 1) % count) for i in range(ends)]),
                cells,
                lax.ppermute(head, axis, [((i + 1) % count, i) for i in range(ends)]),
            ],
            axis=dim,
        )
    return cells


def stencil(padded):
    edges = (
        padded[..., 2:, 1:-1]
        + padded[..., :-2, 1:-1]
        + padded[..., 1:-1, 2:]
        + padded[..., 1:-1, :-2]
    )
    corners = (
        padded[..., 2:, 2:] + padded[..., 2:, :-2] + padded[..., :-2, 2:] + padded[..., :-2, :-2]
    )
    return 4.0 * edges + corners


def pad_columns(field):
    return jnp.pad(field, [(0, 0)] * (field.ndim - 1) + [(1, 1)])


def coefficients(speeds, angular, parity):
    speed_grid = speeds[None, None]
    angular_col = angular[None, :, None, None]
    parity_col = parity[:, None, None, None]
    real_coef = pade_second * (speed_grid / (angular_col * grid_spacing)) ** 2
    imag_coef = (
        -parity_col
        * pade_first
        * layer_thickness
        * speed_grid
        / (2.0 * angular_col * grid_spacing**2)
    )
    return (real_coef, imag_coef)


def phase_screen(fields, speeds, angular, parity):
    phase_angle = (
        parity[:, None, None, None]
        * angular[None, :, None, None]
        * layer_thickness
        / speeds[None, None]
    )
    cosine = jnp.cos(phase_angle)
    sine_part = jnp.sin(phase_angle)
    wave_real = fields[:, 0] * cosine + fields[:, 1] * sine_part
    wave_imag = fields[:, 1] * cosine - fields[:, 0] * sine_part
    return jnp.stack([wave_real, wave_imag], axis=1)


def operator_terms(screened, nearby, real_coef, imag_coef):
    laplace = (nearby - 20.0 * screened) / 6.0
    rhs_real = screened[:, 0] - (real_coef * laplace[:, 0] + imag_coef * laplace[:, 1])
    rhs_imag = screened[:, 1] - (real_coef * laplace[:, 1] - imag_coef * laplace[:, 0])
    diagonal = 6.0 + 20.0 * real_coef
    denominator = diagonal * diagonal + 400.0 * imag_coef * imag_coef
    couple_real = (real_coef * diagonal + 20.0 * imag_coef * imag_coef) / denominator
    couple_imag = 6.0 * imag_coef / denominator
    base_real = 6.0 * (rhs_real * diagonal + 20.0 * imag_coef * rhs_imag) / denominator
    base_imag = 6.0 * (rhs_imag * diagonal - 20.0 * imag_coef * rhs_real) / denominator
    return (base_real, base_imag, couple_real, couple_imag)


def jacobi_update(nearby, terms):
    base_real, base_imag, couple_real, couple_imag = terms
    new_real = base_real + couple_real * nearby[:, 0] - couple_imag * nearby[:, 1]
    new_imag = base_imag + couple_real * nearby[:, 1] + couple_imag * nearby[:, 0]
    return jnp.stack([new_real, new_imag], axis=1)


def image_terms(fields, offsets, width):
    half_offs = offsets // 2
    padded = jnp.pad(fields, [(0, 0)] * 4 + [(half_offs, half_offs)])
    image_rows = []
    for offset in range(offsets):
        source = padded[0, :, :, :, 2 * half_offs - offset : 2 * half_offs - offset + width]
        receiver = padded[1, :, :, :, offset : offset + width]
        image_rows.append(jnp.sum(source[0] * receiver[0] + source[1] * receiver[1], axis=0))
    return jnp.stack(image_rows)


def on_device(wave, velocity):
    freq_dev = wave.shape[2]
    freq_total = freq_dev * lax.axis_size("freq")
    freq_index = (lax.axis_index("freq") * freq_dev + jnp.arange(freq_dev, dtype=jnp.int32)).astype(
        jnp.float32
    )
    angular = full_turn * (8.0 + 48.0 * freq_index / freq_total)
    parity = jnp.array([1.0, -1.0], dtype=jnp.float32)
    fields = wave
    image_parts = []
    for depth_level in range(STEPS):
        screened = phase_screen(fields, velocity[depth_level], angular, parity)
        real_coef, imag_coef = coefficients(velocity[depth_level], angular, parity)
        current = screened
        for sweep_count in range(SWEEPS):
            extended = extended_2(current, (("tile", 3),), 1)
            nearby = stencil(pad_columns(extended))
            if sweep_count == 0:
                terms = operator_terms(current, nearby, real_coef, imag_coef)
            current = jacobi_update(nearby, terms)
        fields = current
        image_part = image_terms(fields, OFFS, fields.shape[4]) * (1.0 / math.sqrt(freq_total))
        image_parts.append(image_part)
    return lax.psum_scatter(jnp.stack(image_parts), "freq", scatter_dimension=1, tiled=True)


def solution(mesh):
    placed = (P(None, None, "freq", "tile", None), P(None, "tile", None))
    return jax.shard_map(
        on_device,
        mesh=mesh,
        in_specs=placed,
        out_specs=P(None, "freq", "tile", None),
        check_vma=False,
    )
```

profile of v0, /device:TPU:0, one launch (start us, length us, event | category | flops | bytes accessed | tf_op | source)
XLA Modules:
  0.0 577.1 jit_solution(3292854509324234785)
XLA Ops:
  7.8 3.8 multiply_add_fusion.26
  11.6 1.3 collective-permute-start
  12.9 5.5 collective-permute-start.1
  24.1 5.4 collective-permute-start.3
  29.6 1.4 collective-permute-done.3
  34.3 5.7 collective-permute-start.5
  40.0 1.4 collective-permute-done.5
  44.7 5.7 collective-permute-start.7
  50.5 1.4 collective-permute-done.7
  53.9 1.3 collective-permute-start.8
  55.2 6.0 %collective-permute-start.9 = (f32[2,2,1,1,1024]{4,3,2,1,0:T(1,128)S(1)}, f32[2,2,1,1,1024]{4,3,2,1,0:T(1,128)S(1)}, u32[]{:S(2)}, u32[]{:S(2)}) collective-permute-start(f32[2,2,1,1,1024]{4,3,2,1,0:T(1,128)S(1)} %get-tuple-element.119), channel_id=1, source_target_pairs={{0,1},{1,2},{2,3},{4,5},{5,6},{6,7},{8,9},{9,10},{10,11},{12,13},{... | collective-permute-start | bytes 49160 | tf_op jit(solution)/shard_map/ppermute | solution.py:28
  65.6 5.8 %collective-permute-start.11 = (f32[2,2,1,1,1024]{4,3,2,1,0:T(1,128)S(1)}, f32[2,2,1,1,1024]{4,3,2,1,0:T(1,128)S(1)}, u32[]{:S(2)}, u32[]{:S(2)}) collective-permute-start(f32[2,2,1,1,1024]{4,3,2,1,0:T(1,128)S(1)} %get-tuple-element.117), channel_id=1, source_target_pairs={{0,1},{1,2},{2,3},{4,5},{5,6},{6,7},{8,9},{9,10},{10,11},{12,13},{... | collective-permute-start | bytes 49160 | tf_op jit(solution)/shard_map/ppermute | solution.py:28
  71.5 1.4 collective-permute-done.11
  76.2 5.7 collective-permute-start.13
  81.9 1.4 collective-permute-done.13
  86.6 5.7 collective-permute-start.15
  92.4 1.3 collective-permute-done.15
  95.3 2.3 multiply_subtract_fusion.17
  98.0 2.1 multiply_add_fusion.17
  104.0 5.7 collective-permute-start.17
  114.2 1.3 collective-permute-start.18
  115.5 5.7 collective-permute-start.19
  124.6 9.9 %collective-permute-start.20 = (f32[2,2,1,1,1024]{4,3,2,1,0:T(1,128)S(1)}, f32[2,2,1,1,1024]{4,3,2,1,0:T(1,128)S(1)}, u32[]{:S(2)}, u32[]{:S(2)}) collective-permute-start(f32[2,2,1,1,1024]{4,3,2,1,0:T(1,128)S(1)} %get-tuple-element.108), channel_id=1, source_target_pairs={{1,0},{2,1},{3,2},{5,4},{6,5},{7,6},{9,8},{10,9},{11,10},{13,12},{... | collective-permute-start | bytes 49160 | tf_op jit(solution)/shard_map/ppermute | solution.py:30
  134.5 5.7 collective-permute-start.21
  143.6 1.3 collective-permute-start.22
  144.9 5.7 collective-permute-start.23
  155.4 5.7 collective-permute-start.25
  165.8 5.8 %collective-permute-start.27 = (f32[2,2,1,1,1024]{4,3,2,1,0:T(1,128)S(1)}, f32[2,2,1,1,1024]{4,3,2,1,0:T(1,128)S(1)}, u32[]{:S(2)}, u32[]{:S(2)}) collective-permute-start(f32[2,2,1,1,1024]{4,3,2,1,0:T(1,128)S(1)} %get-tuple-element.101), channel_id=1, source_target_pairs={{0,1},{1,2},{2,3},{4,5},{5,6},{6,7},{8,9},{9,10},{10,11},{12,13},{... | collective-permute-start | bytes 49160 | tf_op jit(solution)/shard_map/ppermute | solution.py:28
  176.3 5.7 collective-permute-start.29
  186.8 5.9 %collective-permute-start.31 = (f32[2,2,1,1,1024]{4,3,2,1,0:T(1,128)S(1)}, f32[2,2,1,1,1024]{4,3,2,1,0:T(1,128)S(1)}, u32[]{:S(2)}, u32[]{:S(2)}) collective-permute-start(f32[2,2,1,1,1024]{4,3,2,1,0:T(1,128)S(1)} %get-tuple-element.97), channel_id=1, source_target_pairs={{0,1},{1,2},{2,3},{4,5},{5,6},{6,7},{8,9},{9,10},{10,11},{12,13},{... | collective-permute-start | bytes 49160 | tf_op jit(solution)/shard_map/ppermute | solution.py:28
  192.7 2.5 broadcast_multiply_fusion.2
  196.7 2.3 multiply_subtract_fusion.8
  199.4 2.1 multiply_add_fusion.8
  204.1 1.3 collective-permute-start.32
  205.4 5.7 collective-permute-start.33
  211.3 1.4 collective-permute-done.33
  216.9 5.9 %collective-permute-start.35 = (f32[2,2,1,1,1024]{4,3,2,1,0:T(1,128)S(1)}, f32[2,2,1,1,1024]{4,3,2,1,0:T(1,128)S(1)}, u32[]{:S(2)}, u32[]{:S(2)}) collective-permute-start(f32[2,2,1,1,1024]{4,3,2,1,0:T(1,128)S(1)} %get-tuple-element.93), channel_id=1, source_target_pairs={{0,1},{1,2},{2,3},{4,5},{5,6},{6,7},{8,9},{9,10},{10,11},{12,13},{... | collective-permute-start | bytes 49160 | tf_op jit(solution)/shard_map/ppermute | solution.py:28
  227.0 5.7 collective-permute-start.37
  237.5 5.7 collective-permute-start.39
  247.9 5.7 collective-permute-start.41
  258.4 5.7 collective-permute-start.43
  268.8 5.9 %collective-permute-start.45 = (f32[2,2,1,1,1024]{4,3,2,1,0:T(1,128)S(1)}, f32[2,2,1,1,1024]{4,3,2,1,0:T(1,128)S(1)}, u32[]{:S(2)}, u32[]{:S(2)}) collective-permute-start(f32[2,2,1,1,1024]{4,3,2,1,0:T(1,128)S(1)} %get-tuple-element.83), channel_id=1, source_target_pairs={{0,1},{1,2},{2,3},{4,5},{5,6},{6,7},{8,9},{9,10},{10,11},{12,13},{... | collective-permute-start | bytes 49160 | tf_op jit(solution)/shard_map/ppermute | solution.py:28
  278.0 1.3 collective-permute-start.46
  279.3 5.7 collective-permute-start.47
  293.8 4.3 broadcast_multiply_fusion
  298.1 10.3 %pad_maximum_fusion = f32[3,16,64,1024]{3,2,1,0:T(8,128)} fusion(f32[1,16,64,1024]{3,2,1,0:T(8,128)} %get-tuple-element.138, f32[1,16,64,1024]{3,2,1,0:T(8,128)} %get-tuple-element.139, f32[1,16,64,1024]{3,2,1,0:T(8,128)S(1)} %copy-done), kind=kLoop, calls=%fused_computation | loop fusion | flops 6291456 | bytes 25165824 | tf_op jit(solution)/shard_map/stack | solution.py:137
  310.2 257.1 %all-reduce.30.cloned.1.call-done = f32[3,16,64,1024]{3,2,1,0:T(8,128)} async-done(((f32[3,16,64,1024]{3,2,1,0:T(8,128)}), f32[3,16,64,1024]{3,2,1,0:T(8,128)}) %all-reduce.30.cloned.1.call-update) | async-done | bytes 12582928
  567.4 2.7 constant_dynamic-slice_fusion
  (237 shorter events, 106.5 us)
Async XLA Ops:
  6.5 560.8 %all-reduce.30.cloned.1.call-start = ((), (), s32[]{:S(2)}) async-start(), calls=%async_computation | async-start | bytes 25165824
  11.6 8.1 %collective-permute-start = (f32[2,2,1,1,1024]{4,3,2,1,0:T(1,128)S(1)}, f32[2,2,1,1,1024]{4,3,2,1,0:T(1,128)S(1)}, u32[]{:S(2)}, u32[]{:S(2)}) collective-permute-start(f32[2,2,1,1,1024]{4,3,2,1,0:T(1,128)S(1)} %get-tuple-element.128), channel_id=1, source_target_pairs={{1,0},{2,1},{3,2},{5,4},{6,5},{7,6},{9,8},{10,9},{11,10},{13,12},{... | collective-permute-start | bytes 49160 | tf_op jit(solution)/shard_map/ppermute | solution.py:30
  12.9 6.9 %collective-permute-start.1 = (f32[2,2,1,1,1024]{4,3,2,1,0:T(1,128)S(1)}, f32[2,2,1,1,1024]{4,3,2,1,0:T(1,128)S(1)}, u32[]{:S(2)}, u32[]{:S(2)}) collective-permute-start(f32[2,2,1,1,1024]{4,3,2,1,0:T(1,128)S(1)} %get-tuple-element.127), channel_id=1, source_target_pairs={{0,1},{1,2},{2,3},{4,5},{5,6},{6,7},{8,9},{9,10},{10,11},{12,13},{... | collective-permute-start | bytes 49160 | tf_op jit(solution)/shard_map/ppermute | solution.py:28
  24.1 6.9 %collective-permute-start.3 = (f32[2,2,1,1,1024]{4,3,2,1,0:T(1,128)S(1)}, f32[2,2,1,1,1024]{4,3,2,1,0:T(1,128)S(1)}, u32[]{:S(2)}, u32[]{:S(2)}) collective-permute-start(f32[2,2,1,1,1024]{4,3,2,1,0:T(1,128)S(1)} %get-tuple-element.125), channel_id=1, source_target_pairs={{0,1},{1,2},{2,3},{4,5},{5,6},{6,7},{8,9},{9,10},{10,11},{12,13},{... | collective-permute-start | bytes 49160 | tf_op jit(solution)/shard_map/ppermute | solution.py:28
  33.0 7.0 %collective-permute-start.4 = (f32[2,2,1,1,1024]{4,3,2,1,0:T(1,128)S(1)}, f32[2,2,1,1,1024]{4,3,2,1,0:T(1,128)S(1)}, u32[]{:S(2)}, u32[]{:S(2)}) collective-permute-start(f32[2,2,1,1,1024]{4,3,2,1,0:T(1,128)S(1)} %get-tuple-element.124), channel_id=1, source_target_pairs={{1,0},{2,1},{3,2},{5,4},{6,5},{7,6},{9,8},{10,9},{11,10},{13,12},{... | collective-permute-start | bytes 49160 | tf_op jit(solution)/shard_map/ppermute | solution.py:30
  34.3 7.2 %collective-permute-start.5 = (f32[2,2,1,1,1024]{4,3,2,1,0:T(1,128)S(1)}, f32[2,2,1,1,1024]{4,3,2,1,0:T(1,128)S(1)}, u32[]{:S(2)}, u32[]{:S(2)}) collective-permute-start(f32[2,2,1,1,1024]{4,3,2,1,0:T(1,128)S(1)} %get-tuple-element.123), channel_id=1, source_target_pairs={{0,1},{1,2},{2,3},{4,5},{5,6},{6,7},{8,9},{9,10},{10,11},{12,13},{... | collective-permute-start | bytes 49160 | tf_op jit(solution)/shard_map/ppermute | solution.py:28
  43.4 7.0 %collective-permute-start.6 = (f32[2,2,1,1,1024]{4,3,2,1,0:T(1,128)S(1)}, f32[2,2,1,1,1024]{4,3,2,1,0:T(1,128)S(1)}, u32[]{:S(2)}, u32[]{:S(2)}) collective-permute-start(f32[2,2,1,1,1024]{4,3,2,1,0:T(1,128)S(1)} %get-tuple-element.122), channel_id=1, source_target_pairs={{1,0},{2,1},{3,2},{5,4},{6,5},{7,6},{9,8},{10,9},{11,10},{13,12},{... | collective-permute-start | bytes 49160 | tf_op jit(solution)/shard_map/ppermute | solution.py:30
  44.7 7.2 %collective-permute-start.7 = (f32[2,2,1,1,1024]{4,3,2,1,0:T(1,128)S(1)}, f32[2,2,1,1,1024]{4,3,2,1,0:T(1,128)S(1)}, u32[]{:S(2)}, u32[]{:S(2)}) collective-permute-start(f32[2,2,1,1,1024]{4,3,2,1,0:T(1,128)S(1)} %get-tuple-element.121), channel_id=1, source_target_pairs={{0,1},{1,2},{2,3},{4,5},{5,6},{6,7},{8,9},{9,10},{10,11},{12,13},{... | collective-permute-start | bytes 49160 | tf_op jit(solution)/shard_map/ppermute | solution.py:28
  53.9 7.3 %collective-permute-start.8 = (f32[2,2,1,1,1024]{4,3,2,1,0:T(1,128)S(1)}, f32[2,2,1,1,1024]{4,3,2,1,0:T(1,128)S(1)}, u32[]{:S(2)}, u32[]{:S(2)}) collective-permute-start(f32[2,2,1,1,1024]{4,3,2,1,0:T(1,128)S(1)} %get-tuple-element.120), channel_id=1, source_target_pairs={{1,0},{2,1},{3,2},{5,4},{6,5},{7,6},{9,8},{10,9},{11,10},{13,12},{... | collective-permute-start | bytes 49160 | tf_op jit(solution)/shard_map/ppermute | solution.py:30
  55.2 7.2 %collective-permute-start.9 = (f32[2,2,1,1,1024]{4,3,2,1,0:T(1,128)S(1)}, f32[2,2,1,1,1024]{4,3,2,1,0:T(1,128)S(1)}, u32[]{:S(2)}, u32[]{:S(2)}) collective-permute-start(f32[2,2,1,1,1024]{4,3,2,1,0:T(1,128)S(1)} %get-tuple-element.119), channel_id=1, source_target_pairs={{0,1},{1,2},{2,3},{4,5},{5,6},{6,7},{8,9},{9,10},{10,11},{12,13},{... | collective-permute-start | bytes 49160 | tf_op jit(solution)/shard_map/ppermute | solution.py:28
  64.3 7.1 %collective-permute-start.10 = (f32[2,2,1,1,1024]{4,3,2,1,0:T(1,128)S(1)}, f32[2,2,1,1,1024]{4,3,2,1,0:T(1,128)S(1)}, u32[]{:S(2)}, u32[]{:S(2)}) collective-permute-start(f32[2,2,1,1,1024]{4,3,2,1,0:T(1,128)S(1)} %get-tuple-element.118), channel_id=1, source_target_pairs={{1,0},{2,1},{3,2},{5,4},{6,5},{7,6},{9,8},{10,9},{11,10},{13,12},{... | collective-permute-start | bytes 49160 | tf_op jit(solution)/shard_map/ppermute | solution.py:30
  65.6 7.3 %collective-permute-start.11 = (f32[2,2,1,1,1024]{4,3,2,1,0:T(1,128)S(1)}, f32[2,2,1,1,1024]{4,3,2,1,0:T(1,128)S(1)}, u32[]{:S(2)}, u32[]{:S(2)}) collective-permute-start(f32[2,2,1,1,1024]{4,3,2,1,0:T(1,128)S(1)} %get-tuple-element.117), channel_id=1, source_target_pairs={{0,1},{1,2},{2,3},{4,5},{5,6},{6,7},{8,9},{9,10},{10,11},{12,13},{... | collective-permute-start | bytes 49160 | tf_op jit(solution)/shard_map/ppermute | solution.py:28
  74.9 7.0 %collective-permute-start.12 = (f32[2,2,1,1,1024]{4,3,2,1,0:T(1,128)S(1)}, f32[2,2,1,1,1024]{4,3,2,1,0:T(1,128)S(1)}, u32[]{:S(2)}, u32[]{:S(2)}) collective-permute-start(f32[2,2,1,1,1024]{4,3,2,1,0:T(1,128)S(1)} %get-tuple-element.116), channel_id=1, source_target_pairs={{1,0},{2,1},{3,2},{5,4},{6,5},{7,6},{9,8},{10,9},{11,10},{13,12},{... | collective-permute-start | bytes 49160 | tf_op jit(solution)/shard_map/ppermute | solution.py:30
  76.2 7.2 %collective-permute-start.13 = (f32[2,2,1,1,1024]{4,3,2,1,0:T(1,128)S(1)}, f32[2,2,1,1,1024]{4,3,2,1,0:T(1,128)S(1)}, u32[]{:S(2)}, u32[]{:S(2)}) collective-permute-start(f32[2,2,1,1,1024]{4,3,2,1,0:T(1,128)S(1)} %get-tuple-element.115), channel_id=1, source_target_pairs={{0,1},{1,2},{2,3},{4,5},{5,6},{6,7},{8,9},{9,10},{10,11},{12,13},{... | collective-permute-start | bytes 49160 | tf_op jit(solution)/shard_map/ppermute | solution.py:28
  85.3 7.1 %collective-permute-start.14 = (f32[2,2,1,1,1024]{4,3,2,1,0:T(1,128)S(1)}, f32[2,2,1,1,1024]{4,3,2,1,0:T(1,128)S(1)}, u32[]{:S(2)}, u32[]{:S(2)}) collective-permute-start(f32[2,2,1,1,1024]{4,3,2,1,0:T(1,128)S(1)} %get-tuple-element.114), channel_id=1, source_target_pairs={{1,0},{2,1},{3,2},{5,4},{6,5},{7,6},{9,8},{10,9},{11,10},{13,12},{... | collective-permute-start | bytes 49160 | tf_op jit(solution)/shard_map/ppermute | solution.py:30
  86.6 7.2 %collective-permute-start.15 = (f32[2,2,1,1,1024]{4,3,2,1,0:T(1,128)S(1)}, f32[2,2,1,1,1024]{4,3,2,1,0:T(1,128)S(1)}, u32[]{:S(2)}, u32[]{:S(2)}) collective-permute-start(f32[2,2,1,1,1024]{4,3,2,1,0:T(1,128)S(1)} %get-tuple-element.113), channel_id=1, source_target_pairs={{0,1},{1,2},{2,3},{4,5},{5,6},{6,7},{8,9},{9,10},{10,11},{12,13},{... | collective-permute-start | bytes 49160 | tf_op jit(solution)/shard_map/ppermute | solution.py:28
  102.7 7.4 %collective-permute-start.16 = (f32[2,2,1,1,1024]{4,3,2,1,0:T(1,128)S(1)}, f32[2,2,1,1,1024]{4,3,2,1,0:T(1,128)S(1)}, u32[]{:S(2)}, u32[]{:S(2)}) collective-permute-start(f32[2,2,1,1,1024]{4,3,2,1,0:T(1,128)S(1)} %get-tuple-element.112), channel_id=1, source_target_pairs={{1,0},{2,1},{3,2},{5,4},{6,5},{7,6},{9,8},{10,9},{11,10},{13,12},{... | collective-permute-start | bytes 49160 | tf_op jit(solution)/shard_map/ppermute | solution.py:30
  104.0 7.2 %collective-permute-start.17 = (f32[2,2,1,1,1024]{4,3,2,1,0:T(1,128)S(1)}, f32[2,2,1,1,1024]{4,3,2,1,0:T(1,128)S(1)}, u32[]{:S(2)}, u32[]{:S(2)}) collective-permute-start(f32[2,2,1,1,1024]{4,3,2,1,0:T(1,128)S(1)} %get-tuple-element.111), channel_id=1, source_target_pairs={{0,1},{1,2},{2,3},{4,5},{5,6},{6,7},{8,9},{9,10},{10,11},{12,13},{... | collective-permute-start | bytes 49160 | tf_op jit(solution)/shard_map/ppermute | solution.py:28
  114.2 7.4 %collective-permute-start.18 = (f32[2,2,1,1,1024]{4,3,2,1,0:T(1,128)S(1)}, f32[2,2,1,1,1024]{4,3,2,1,0:T(1,128)S(1)}, u32[]{:S(2)}, u32[]{:S(2)}) collective-permute-start(f32[2,2,1,1,1024]{4,3,2,1,0:T(1,128)S(1)} %get-tuple-element.110), channel_id=1, source_target_pairs={{1,0},{2,1},{3,2},{5,4},{6,5},{7,6},{9,8},{10,9},{11,10},{13,12},{... | collective-permute-start | bytes 49160 | tf_op jit(solution)/shard_map/ppermute | solution.py:30
  115.5 7.2 %collective-permute-start.19 = (f32[2,2,1,1,1024]{4,3,2,1,0:T(1,128)S(1)}, f32[2,2,1,1,1024]{4,3,2,1,0:T(1,128)S(1)}, u32[]{:S(2)}, u32[]{:S(2)}) collective-permute-start(f32[2,2,1,1,1024]{4,3,2,1,0:T(1,128)S(1)} %get-tuple-element.109), channel_id=1, source_target_pairs={{0,1},{1,2},{2,3},{4,5},{5,6},{6,7},{8,9},{9,10},{10,11},{12,13},{... | collective-permute-start | bytes 49160 | tf_op jit(solution)/shard_map/ppermute | solution.py:28
  124.6 16.0 %collective-permute-start.20 = (f32[2,2,1,1,1024]{4,3,2,1,0:T(1,128)S(1)}, f32[2,2,1,1,1024]{4,3,2,1,0:T(1,128)S(1)}, u32[]{:S(2)}, u32[]{:S(2)}) collective-permute-start(f32[2,2,1,1,1024]{4,3,2,1,0:T(1,128)S(1)} %get-tuple-element.108), channel_id=1, source_target_pairs={{1,0},{2,1},{3,2},{5,4},{6,5},{7,6},{9,8},{10,9},{11,10},{13,12},{... | collective-permute-start | bytes 49160 | tf_op jit(solution)/shard_map/ppermute | solution.py:30
  134.5 7.2 %collective-permute-start.21 = (f32[2,2,1,1,1024]{4,3,2,1,0:T(1,128)S(1)}, f32[2,2,1,1,1024]{4,3,2,1,0:T(1,128)S(1)}, u32[]{:S(2)}, u32[]{:S(2)}) collective-permute-start(f32[2,2,1,1,1024]{4,3,2,1,0:T(1,128)S(1)} %get-tuple-element.107), channel_id=1, source_target_pairs={{0,1},{1,2},{2,3},{4,5},{5,6},{6,7},{8,9},{9,10},{10,11},{12,13},{... | collective-permute-start | bytes 49160 | tf_op jit(solution)/shard_map/ppermute | solution.py:28
  143.6 7.4 %collective-permute-start.22 = (f32[2,2,1,1,1024]{4,3,2,1,0:T(1,128)S(1)}, f32[2,2,1,1,1024]{4,3,2,1,0:T(1,128)S(1)}, u32[]{:S(2)}, u32[]{:S(2)}) collective-permute-start(f32[2,2,1,1,1024]{4,3,2,1,0:T(1,128)S(1)} %get-tuple-element.106), channel_id=1, source_target_pairs={{1,0},{2,1},{3,2},{5,4},{6,5},{7,6},{9,8},{10,9},{11,10},{13,12},{... | collective-permute-start | bytes 49160 | tf_op jit(solution)/shard_map/ppermute | solution.py:30
  144.9 7.2 %collective-permute-start.23 = (f32[2,2,1,1,1024]{4,3,2,1,0:T(1,128)S(1)}, f32[2,2,1,1,1024]{4,3,2,1,0:T(1,128)S(1)}, u32[]{:S(2)}, u32[]{:S(2)}) collective-permute-start(f32[2,2,1,1,1024]{4,3,2,1,0:T(1,128)S(1)} %get-tuple-element.105), channel_id=1, source_target_pairs={{0,1},{1,2},{2,3},{4,5},{5,6},{6,7},{8,9},{9,10},{10,11},{12,13},{... | collective-permute-start | bytes 49160 | tf_op jit(solution)/shard_map/ppermute | solution.py:28
  154.1 7.4 %collective-permute-start.24 = (f32[2,2,1,1,1024]{4,3,2,1,0:T(1,128)S(1)}, f32[2,2,1,1,1024]{4,3,2,1,0:T(1,128)S(1)}, u32[]{:S(2)}, u32[]{:S(2)}) collective-permute-start(f32[2,2,1,1,1024]{4,3,2,1,0:T(1,128)S(1)} %get-tuple-element.104), channel_id=1, source_target_pairs={{1,0},{2,1},{3,2},{5,4},{6,5},{7,6},{9,8},{10,9},{11,10},{13,12},{... | collective-permute-start | bytes 49160 | tf_op jit(solution)/shard_map/ppermute | solution.py:30
  155.4 7.2 %collective-permute-start.25 = (f32[2,2,1,1,1024]{4,3,2,1,0:T(1,128)S(1)}, f32[2,2,1,1,1024]{4,3,2,1,0:T(1,128)S(1)}, u32[]{:S(2)}, u32[]{:S(2)}) collective-permute-start(f32[2,2,1,1,1024]{4,3,2,1,0:T(1,128)S(1)} %get-tuple-element.103), channel_id=1, source_target_pairs={{0,1},{1,2},{2,3},{4,5},{5,6},{6,7},{8,9},{9,10},{10,11},{12,13},{... | collective-permute-start | bytes 49160 | tf_op jit(solution)/shard_map/ppermute | solution.py:28
  164.5 7.5 %collective-permute-start.26 = (f32[2,2,1,1,1024]{4,3,2,1,0:T(1,128)S(1)}, f32[2,2,1,1,1024]{4,3,2,1,0:T(1,128)S(1)}, u32[]{:S(2)}, u32[]{:S(2)}) collective-permute-start(f32[2,2,1,1,1024]{4,3,2,1,0:T(1,128)S(1)} %get-tuple-element.102), channel_id=1, source_target_pairs={{1,0},{2,1},{3,2},{5,4},{6,5},{7,6},{9,8},{10,9},{11,10},{13,12},{... | collective-permute-start | bytes 49160 | tf_op jit(solution)/shard_map/ppermute | solution.py:30
  165.8 7.3 %collective-permute-start.27 = (f32[2,2,1,1,1024]{4,3,2,1,0:T(1,128)S(1)}, f32[2,2,1,1,1024]{4,3,2,1,0:T(1,128)S(1)}, u32[]{:S(2)}, u32[]{:S(2)}) collective-permute-start(f32[2,2,1,1,1024]{4,3,2,1,0:T(1,128)S(1)} %get-tuple-element.101), channel_id=1, source_target_pairs={{0,1},{1,2},{2,3},{4,5},{5,6},{6,7},{8,9},{9,10},{10,11},{12,13},{... | collective-permute-start | bytes 49160 | tf_op jit(solution)/shard_map/ppermute | solution.py:28
  175.0 7.4 %collective-permute-start.28 = (f32[2,2,1,1,1024]{4,3,2,1,0:T(1,128)S(1)}, f32[2,2,1,1,1024]{4,3,2,1,0:T(1,128)S(1)}, u32[]{:S(2)}, u32[]{:S(2)}) collective-permute-start(f32[2,2,1,1,1024]{4,3,2,1,0:T(1,128)S(1)} %get-tuple-element.100), channel_id=1, source_target_pairs={{1,0},{2,1},{3,2},{5,4},{6,5},{7,6},{9,8},{10,9},{11,10},{13,12},{... | collective-permute-start | bytes 49160 | tf_op jit(solution)/shard_map/ppermute | solution.py:30
  176.3 7.2 %collective-permute-start.29 = (f32[2,2,1,1,1024]{4,3,2,1,0:T(1,128)S(1)}, f32[2,2,1,1,1024]{4,3,2,1,0:T(1,128)S(1)}, u32[]{:S(2)}, u32[]{:S(2)}) collective-permute-start(f32[2,2,1,1,1024]{4,3,2,1,0:T(1,128)S(1)} %get-tuple-element.99), channel_id=1, source_target_pairs={{0,1},{1,2},{2,3},{4,5},{5,6},{6,7},{8,9},{9,10},{10,11},{12,13},{... | collective-permute-start | bytes 49160 | tf_op jit(solution)/shard_map/ppermute | solution.py:28
  185.5 9.8 %collective-permute-start.30 = (f32[2,2,1,1,1024]{4,3,2,1,0:T(1,128)S(1)}, f32[2,2,1,1,1024]{4,3,2,1,0:T(1,128)S(1)}, u32[]{:S(2)}, u32[]{:S(2)}) collective-permute-start(f32[2,2,1,1,1024]{4,3,2,1,0:T(1,128)S(1)} %get-tuple-element.98), channel_id=1, source_target_pairs={{1,0},{2,1},{3,2},{5,4},{6,5},{7,6},{9,8},{10,9},{11,10},{13,12},{... | collective-permute-start | bytes 49160 | tf_op jit(solution)/shard_map/ppermute | solution.py:30
  186.8 8.5 %collective-permute-start.31 = (f32[2,2,1,1,1024]{4,3,2,1,0:T(1,128)S(1)}, f32[2,2,1,1,1024]{4,3,2,1,0:T(1,128)S(1)}, u32[]{:S(2)}, u32[]{:S(2)}) collective-permute-start(f32[2,2,1,1,1024]{4,3,2,1,0:T(1,128)S(1)} %get-tuple-element.97), channel_id=1, source_target_pairs={{0,1},{1,2},{2,3},{4,5},{5,6},{6,7},{8,9},{9,10},{10,11},{12,13},{... | collective-permute-start | bytes 49160 | tf_op jit(solution)/shard_map/ppermute | solution.py:28
  204.1 7.1 %collective-permute-start.32 = (f32[2,2,1,1,1024]{4,3,2,1,0:T(1,128)S(1)}, f32[2,2,1,1,1024]{4,3,2,1,0:T(1,128)S(1)}, u32[]{:S(2)}, u32[]{:S(2)}) collective-permute-start(f32[2,2,1,1,1024]{4,3,2,1,0:T(1,128)S(1)} %get-tuple-element.96), channel_id=1, source_target_pairs={{1,0},{2,1},{3,2},{5,4},{6,5},{7,6},{9,8},{10,9},{11,10},{13,12},{... | collective-permute-start | bytes 49160 | tf_op jit(solution)/shard_map/ppermute | solution.py:30
  205.4 7.2 %collective-permute-start.33 = (f32[2,2,1,1,1024]{4,3,2,1,0:T(1,128)S(1)}, f32[2,2,1,1,1024]{4,3,2,1,0:T(1,128)S(1)}, u32[]{:S(2)}, u32[]{:S(2)}) collective-permute-start(f32[2,2,1,1,1024]{4,3,2,1,0:T(1,128)S(1)} %get-tuple-element.95), channel_id=1, source_target_pairs={{0,1},{1,2},{2,3},{4,5},{5,6},{6,7},{8,9},{9,10},{10,11},{12,13},{... | collective-permute-start | bytes 49160 | tf_op jit(solution)/shard_map/ppermute | solution.py:28
  215.6 7.5 %collective-permute-start.34 = (f32[2,2,1,1,1024]{4,3,2,1,0:T(1,128)S(1)}, f32[2,2,1,1,1024]{4,3,2,1,0:T(1,128)S(1)}, u32[]{:S(2)}, u32[]{:S(2)}) collective-permute-start(f32[2,2,1,1,1024]{4,3,2,1,0:T(1,128)S(1)} %get-tuple-element.94), channel_id=1, source_target_pairs={{1,0},{2,1},{3,2},{5,4},{6,5},{7,6},{9,8},{10,9},{11,10},{13,12},{... | collective-permute-start | bytes 49160 | tf_op jit(solution)/shard_map/ppermute | solution.py:30
  216.9 6.9 %collective-permute-start.35 = (f32[2,2,1,1,1024]{4,3,2,1,0:T(1,128)S(1)}, f32[2,2,1,1,1024]{4,3,2,1,0:T(1,128)S(1)}, u32[]{:S(2)}, u32[]{:S(2)}) collective-permute-start(f32[2,2,1,1,1024]{4,3,2,1,0:T(1,128)S(1)} %get-tuple-element.93), channel_id=1, source_target_pairs={{0,1},{1,2},{2,3},{4,5},{5,6},{6,7},{8,9},{9,10},{10,11},{12,13},{... | collective-permute-start | bytes 49160 | tf_op jit(solution)/shard_map/ppermute | solution.py:28
  225.7 7.4 %collective-permute-start.36 = (f32[2,2,1,1,1024]{4,3,2,1,0:T(1,128)S(1)}, f32[2,2,1,1,1024]{4,3,2,1,0:T(1,128)S(1)}, u32[]{:S(2)}, u32[]{:S(2)}) collective-permute-start(f32[2,2,1,1,1024]{4,3,2,1,0:T(1,128)S(1)} %get-tuple-element.92), channel_id=1, source_target_pairs={{1,0},{2,1},{3,2},{5,4},{6,5},{7,6},{9,8},{10,9},{11,10},{13,12},{... | collective-permute-start | bytes 49160 | tf_op jit(solution)/shard_map/ppermute | solution.py:30
  227.0 7.2 %collective-permute-start.37 = (f32[2,2,1,1,1024]{4,3,2,1,0:T(1,128)S(1)}, f32[2,2,1,1,1024]{4,3,2,1,0:T(1,128)S(1)}, u32[]{:S(2)}, u32[]{:S(2)}) collective-permute-start(f32[2,2,1,1,1024]{4,3,2,1,0:T(1,128)S(1)} %get-tuple-element.91), channel_id=1, source_target_pairs={{0,1},{1,2},{2,3},{4,5},{5,6},{6,7},{8,9},{9,10},{10,11},{12,13},{... | collective-permute-start | bytes 49160 | tf_op jit(solution)/shard_map/ppermute | solution.py:28
  236.2 7.4 %collective-permute-start.38 = (f32[2,2,1,1,1024]{4,3,2,1,0:T(1,128)S(1)}, f32[2,2,1,1,1024]{4,3,2,1,0:T(1,128)S(1)}, u32[]{:S(2)}, u32[]{:S(2)}) collective-permute-start(f32[2,2,1,1,1024]{4,3,2,1,0:T(1,128)S(1)} %get-tuple-element.90), channel_id=1, source_target_pairs={{1,0},{2,1},{3,2},{5,4},{6,5},{7,6},{9,8},{10,9},{11,10},{13,12},{... | collective-permute-start | bytes 49160 | tf_op jit(solution)/shard_map/ppermute | solution.py:30
  237.5 7.2 %collective-permute-start.39 = (f32[2,2,1,1,1024]{4,3,2,1,0:T(1,128)S(1)}, f32[2,2,1,1,1024]{4,3,2,1,0:T(1,128)S(1)}, u32[]{:S(2)}, u32[]{:S(2)}) collective-permute-start(f32[2,2,1,1,1024]{4,3,2,1,0:T(1,128)S(1)} %get-tuple-element.89), channel_id=1, source_target_pairs={{0,1},{1,2},{2,3},{4,5},{5,6},{6,7},{8,9},{9,10},{10,11},{12,13},{... | collective-permute-start | bytes 49160 | tf_op jit(solution)/shard_map/ppermute | solution.py:28
  246.6 7.4 %collective-permute-start.40 = (f32[2,2,1,1,1024]{4,3,2,1,0:T(1,128)S(1)}, f32[2,2,1,1,1024]{4,3,2,1,0:T(1,128)S(1)}, u32[]{:S(2)}, u32[]{:S(2)}) collective-permute-start(f32[2,2,1,1,1024]{4,3,2,1,0:T(1,128)S(1)} %get-tuple-element.88), channel_id=1, source_target_pairs={{1,0},{2,1},{3,2},{5,4},{6,5},{7,6},{9,8},{10,9},{11,10},{13,12},{... | collective-permute-start | bytes 49160 | tf_op jit(solution)/shard_map/ppermute | solution.py:30
  247.9 7.2 %collective-permute-start.41 = (f32[2,2,1,1,1024]{4,3,2,1,0:T(1,128)S(1)}, f32[2,2,1,1,1024]{4,3,2,1,0:T(1,128)S(1)}, u32[]{:S(2)}, u32[]{:S(2)}) collective-permute-start(f32[2,2,1,1,1024]{4,3,2,1,0:T(1,128)S(1)} %get-tuple-element.87), channel_id=1, source_target_pairs={{0,1},{1,2},{2,3},{4,5},{5,6},{6,7},{8,9},{9,10},{10,11},{12,13},{... | collective-permute-start | bytes 49160 | tf_op jit(solution)/shard_map/ppermute | solution.py:28
  257.1 7.4 %collective-permute-start.42 = (f32[2,2,1,1,1024]{4,3,2,1,0:T(1,128)S(1)}, f32[2,2,1,1,1024]{4,3,2,1,0:T(1,128)S(1)}, u32[]{:S(2)}, u32[]{:S(2)}) collective-permute-start(f32[2,2,1,1,1024]{4,3,2,1,0:T(1,128)S(1)} %get-tuple-element.86), channel_id=1, source_target_pairs={{1,0},{2,1},{3,2},{5,4},{6,5},{7,6},{9,8},{10,9},{11,10},{13,12},{... | collective-permute-start | bytes 49160 | tf_op jit(solution)/shard_map/ppermute | solution.py:30
  258.4 7.2 %collective-permute-start.43 = (f32[2,2,1,1,1024]{4,3,2,1,0:T(1,128)S(1)}, f32[2,2,1,1,1024]{4,3,2,1,0:T(1,128)S(1)}, u32[]{:S(2)}, u32[]{:S(2)}) collective-permute-start(f32[2,2,1,1,1024]{4,3,2,1,0:T(1,128)S(1)} %get-tuple-element.85), channel_id=1, source_target_pairs={{0,1},{1,2},{2,3},{4,5},{5,6},{6,7},{8,9},{9,10},{10,11},{12,13},{... | collective-permute-start | bytes 49160 | tf_op jit(solution)/shard_map/ppermute | solution.py:28
  267.5 7.5 %collective-permute-start.44 = (f32[2,2,1,1,1024]{4,3,2,1,0:T(1,128)S(1)}, f32[2,2,1,1,1024]{4,3,2,1,0:T(1,128)S(1)}, u32[]{:S(2)}, u32[]{:S(2)}) collective-permute-start(f32[2,2,1,1,1024]{4,3,2,1,0:T(1,128)S(1)} %get-tuple-element.84), channel_id=1, source_target_pairs={{1,0},{2,1},{3,2},{5,4},{6,5},{7,6},{9,8},{10,9},{11,10},{13,12},{... | collective-permute-start | bytes 49160 | tf_op jit(solution)/shard_map/ppermute | solution.py:30
  268.8 7.2 %collective-permute-start.45 = (f32[2,2,1,1,1024]{4,3,2,1,0:T(1,128)S(1)}, f32[2,2,1,1,1024]{4,3,2,1,0:T(1,128)S(1)}, u32[]{:S(2)}, u32[]{:S(2)}) collective-permute-start(f32[2,2,1,1,1024]{4,3,2,1,0:T(1,128)S(1)} %get-tuple-element.83), channel_id=1, source_target_pairs={{0,1},{1,2},{2,3},{4,5},{5,6},{6,7},{8,9},{9,10},{10,11},{12,13},{... | collective-permute-start | bytes 49160 | tf_op jit(solution)/shard_map/ppermute | solution.py:28
  278.0 7.4 %collective-permute-start.46 = (f32[2,2,1,1,1024]{4,3,2,1,0:T(1,128)S(1)}, f32[2,2,1,1,1024]{4,3,2,1,0:T(1,128)S(1)}, u32[]{:S(2)}, u32[]{:S(2)}) collective-permute-start(f32[2,2,1,1,1024]{4,3,2,1,0:T(1,128)S(1)} %get-tuple-element.82), channel_id=1, source_target_pairs={{1,0},{2,1},{3,2},{5,4},{6,5},{7,6},{9,8},{10,9},{11,10},{13,12},{... | collective-permute-start | bytes 49160 | tf_op jit(solution)/shard_map/ppermute | solution.py:30
  279.3 7.2 %collective-permute-start.47 = (f32[2,2,1,1,1024]{4,3,2,1,0:T(1,128)S(1)}, f32[2,2,1,1,1024]{4,3,2,1,0:T(1,128)S(1)}, u32[]{:S(2)}, u32[]{:S(2)}) collective-permute-start(f32[2,2,1,1,1024]{4,3,2,1,0:T(1,128)S(1)} %get-tuple-element.81), channel_id=1, source_target_pairs={{0,1},{1,2},{2,3},{4,5},{5,6},{6,7},{8,9},{9,10},{10,11},{12,13},{... | collective-permute-start | bytes 49160 | tf_op jit(solution)/shard_map/ppermute | solution.py:28
  (12 other events, 32.4 us)
Sparse Core Ops, SparseCore 0:
  308.5 258.8 all-reduce.29
where the time goes:
time: 588 us; the launch traced here: 577 us
  waiting for transfers between devices  283 us (48%)
  starting transfers between devices  177 us (30%)
  other arithmetic  96 us (16%)
  between operations  15.8 us (3%)
    unnamed x2, waiting for transfers between devices  257 us
    ppermute x24, starting transfers between devices, extended_2(): lax.ppermute(tail, axis, [(i, (i + 1) % count) for i in range(ends)])  138 us
    ppermute x24, starting transfers between devices, extended_2(): lax.ppermute(head, axis, [((i + 1) % count, i) for i in range(ends)])  39.6 us
    ppermute x24, waiting for transfers between devices, extended_2(): lax.ppermute(tail, axis, [(i, (i + 1) % count) for i in range(ends)])  25.5 us
    add x21, other arithmetic, stencil(): return 4.0 * edges + corners  20.9 us
    unnamed x45, other arithmetic  14 us
    concatenate x24, other arithmetic, extended_2(): jnp.concatenate([lax.ppermute(tail, axis, [(i, (i + 1) % count) for i in...  11.8 us
  transfers between devices with their start and end apart: 49, of which 24 were waited for; matrix products, arithmetic and copies ran while one was open for 2% of the time, Pallas kernels for 0%

commit v1 on v0

v1 whole, which is shorter than its diff:
```python
import functools
import math

import jax
import jax.numpy as jnp
from jax import lax
from jax.experimental import pallas as pl
from jax.experimental.pallas import tpu as pltpu
from jax.sharding import PartitionSpec as P

STEPS = 3
SWEEPS = 8
OFFS = 16
HALO = 8
LANES = 128

pade_first = 0.376393
pade_second = 0.478242
layer_thickness = 10.0
grid_spacing = 15.0
full_turn = 2.0 * math.pi
angle_mid = 1.2
MESH = pl.DeviceIdType.MESH


def cos_sin(angle):
    y = angle - angle_mid
    z = y * y
    sine = -1.0 / math.factorial(11)
    for power in (9, 7, 5, 3, 1):
        sine = sine * z + (-1.0) ** (power // 2) / math.factorial(power)
    sine = sine * y
    cosine = 1.0 / math.factorial(12)
    for power in (10, 8, 6, 4, 2, 0):
        cosine = cosine * z + (-1.0) ** (power // 2) / math.factorial(power)
    mid_cos, mid_sin = math.cos(angle_mid), math.sin(angle_mid)
    return cosine * mid_cos - sine * mid_sin, sine * mid_cos + cosine * mid_sin


def kernel(
    n, tiles, group, wave_ref, velocity_ref, out_ref, nat, halo, vel, cur, base, coup, recv, img, part,
    vel_sems, halo_sems, field_send, field_recv, image_send, image_recv,
):
    rows, width = velocity_ref.shape[1:]
    cols = width // LANES
    ext = rows + 2 * HALO
    count = ext // 8
    chunk = rows // group
    groups = n // group
    per_dev = OFFS // n
    me = lax.axis_index("freq")
    tile = lax.axis_index("tile")
    my_group, member = me // group, me % group
    has_up, has_down = tile > 0, tile < tiles - 1

    lane = lax.broadcasted_iota(jnp.int32, (8, LANES), 1)
    sub = lax.broadcasted_iota(jnp.int32, (8, LANES), 0)
    angular = full_turn * (8.0 + 48.0 * jnp.full((8, LANES), me, jnp.int32).astype(jnp.float32) / n)
    zero = jnp.zeros((8, LANES), jnp.float32)

    def strided(i):
        return pl.ds(i, 8, stride=count)

    def row_valid(i):
        row = sub * count + (i - HALO + tile * rows)
        return (row >= 0) & (row < tiles * rows)

    def stage(k, _):
        top = pl.multiple_of(k * 8, 8)
        for j in range(cols):
            at = pl.ds(j * LANES, LANES)
            for c in range(4):
                nat[0, c, j, pl.ds(top + HALO, 8), :] = wave_ref[c // 2, c % 2, 0, pl.ds(top, 8), at]
            for d in range(STEPS):
                vel[d, j, pl.ds(top + HALO, 8), :] = velocity_ref[d, pl.ds(top, 8), at]
        return 0

    lax.fori_loop(0, rows // 8, stage, 0)

    barrier = pltpu.get_barrier_semaphore()
    for k in range(1, n):
        pl.semaphore_signal(barrier, inc=1, device_id={"freq": (me + k) % n}, device_id_type=MESH)

    @pl.when(has_up)
    def _():
        pl.semaphore_signal(barrier, inc=1, device_id={"tile": tile - 1}, device_id_type=MESH)

    @pl.when(has_down)
    def _():
        pl.semaphore_signal(barrier, inc=1, device_id={"tile": tile + 1}, device_id_type=MESH)

    near = (tile + tiles - 1) // tiles + (2 * tiles - 2 - tile) // tiles
    pl.semaphore_wait(barrier, n - 1 + near)

    def halo_copy(d, side):
        start = HALO if side == 0 else rows
        return pltpu.make_async_remote_copy(
            src_ref=nat.at[d, :, :, pl.ds(start, HALO), :],
            dst_ref=halo.at[d, side],
            send_sem=halo_sems.at[0, d, side],
            recv_sem=halo_sems.at[1, d, side],
            device_id={"tile": tile - 1 if side == 0 else tile + 1},
            device_id_type=MESH,
        )

    def vel_copy(side):
        start = HALO if side == 0 else rows
        land = rows + HALO if side == 0 else 0
        return pltpu.make_async_remote_copy(
            src_ref=vel.at[:, :, pl.ds(start, HALO), :],
            dst_ref=vel.at[:, :, pl.ds(land, HALO), :],
            send_sem=vel_sems.at[0, side],
            recv_sem=vel_sems.at[1, side],
            device_id={"tile": tile - 1 if side == 0 else tile + 1},
            device_id_type=MESH,
        )

    def field_copy(d, k, sender):
        peer = (member + k) % group
        return pltpu.make_async_remote_copy(
            src_ref=nat.at[d + 1, :, :, pl.ds(pl.multiple_of(HALO + peer * chunk, 8), chunk), :],
            dst_ref=recv.at[d, sender],
            send_sem=field_send.at[d, k],
            recv_sem=field_recv.at[d, sender],
            device_id={"freq": my_group * group + peer},
            device_id_type=MESH,
        )

    def image_copy(d, k, sender):
        peer = (me + k) % n
        top = pl.multiple_of((sender % group) * chunk, 8)
        return pltpu.make_async_remote_copy(
            src_ref=img.at[d, pl.ds(peer * per_dev, per_dev)],
            dst_ref=part.at[d, sender // group, :, pl.ds(top, chunk), :],
            send_sem=image_send.at[d, k],
            recv_sem=image_recv.at[d, sender],
            device_id={"freq": peer},
            device_id_type=MESH,
        )

    def send_halos(d):
        @pl.when(has_up)
        def _():
            halo_copy(d, 0).start()

        @pl.when(has_down)
        def _():
            halo_copy(d, 1).start()

    def take_halos(d):
        @pl.when(has_up)
        def _():
            halo_copy(d, 1).wait_recv()
            for c in range(4):
                for j in range(cols):
                    nat[d, c, j, 0:HALO, :] = halo[d, 1, c, j]

        @pl.when(has_down)
        def _():
            halo_copy(d, 0).wait_recv()
            for c in range(4):
                for j in range(cols):
                    nat[d, c, j, rows + HALO : rows + 2 * HALO, :] = halo[d, 0, c, j]

    @pl.when(has_up)
    def _():
        vel_copy(0).start()

    @pl.when(has_down)
    def _():
        vel_copy(1).start()

    send_halos(0)

    @pl.when(has_up)
    def _():
        vel_copy(1).wait_recv()

    @pl.when(has_down)
    def _():
        vel_copy(0).wait_recv()

    def wrap_rows(slot):
        for c in range(4):
            for j in range(cols):
                cur[slot, c, 0, j] = pltpu.roll(cur[slot, c, count, j], 1, 0)
                cur[slot, c, count + 1, j] = pltpu.roll(cur[slot, c, 1, j], 7, 0)

    def quarter_stencil(slot, c, i):
        sums, to_right, to_left = [], [], []
        for j in range(cols):
            pair = cur[slot, c, i, j] + cur[slot, c, i + 2, j]
            mixed = cur[slot, c, i + 1, j] + 0.25 * pair
            sums.append(pair)
            to_right.append(pltpu.roll(mixed, 1, 1))
            to_left.append(pltpu.roll(mixed, LANES - 1, 1))
        out = []
        for j in range(cols):
            left = jnp.where(lane == 0, to_right[j - 1] if j else zero, to_right[j])
            right = jnp.where(lane == LANES - 1, to_left[j + 1] if j < cols - 1 else zero, to_left[j])
            out.append(sums[j] + (left + right))
        return out

    def depth_step(d):
        take_halos(d)

        def screen(i, _):
            valid = row_valid(i)
            for j in range(cols):
                cosine, sine = cos_sin(angular * layer_thickness / vel[d, j, strided(i), :])
                sr, si, rr, ri = [nat[d, c, j, strided(i), :] for c in range(4)]
                cur[0, 0, i + 1, j] = jnp.where(valid, sr * cosine + si * sine, 0.0)
                cur[0, 1, i + 1, j] = jnp.where(valid, si * cosine - sr * sine, 0.0)
                cur[0, 2, i + 1, j] = jnp.where(valid, rr * cosine - ri * sine, 0.0)
                cur[0, 3, i + 1, j] = jnp.where(valid, ri * cosine + rr * sine, 0.0)
            return 0

        lax.fori_loop(0, count, screen, 0)
        wrap_rows(0)

        def first(i, _):
            valid = row_valid(i)
            for field in range(2):
                near_r = quarter_stencil(0, 2 * field, i)
                near_i = quarter_stencil(0, 2 * field + 1, i)
                for j in range(cols):
                    speed = vel[d, j, strided(i), :]
                    real = pade_second * (speed / (angular * grid_spacing)) ** 2
                    imag = -pade_first * layer_thickness * speed / (2.0 * angular * grid_spacing**2)
                    if field:
                        imag = -imag
                    diag = 6.0 + 20.0 * real
                    inverse = 1.0 / (diag * diag + 400.0 * imag * imag)
                    couple_r = jnp.where(valid, 4.0 * (real * diag + 20.0 * imag * imag) * inverse, 0.0)
                    couple_i = jnp.where(valid, 24.0 * imag * inverse, 0.0)
                    u_r, u_i = cur[0, 2 * field, i + 1, j], cur[0, 2 * field + 1, i + 1, j]
                    lap_r = (4.0 * near_r[j] - 20.0 * u_r) * (1.0 / 6.0)
                    lap_i = (4.0 * near_i[j] - 20.0 * u_i) * (1.0 / 6.0)
                    rhs_r = u_r - (real * lap_r + imag * lap_i)
                    rhs_i = u_i - (real * lap_i - imag * lap_r)
                    base_r = jnp.where(valid, 6.0 * (rhs_r * diag + 20.0 * imag * rhs_i) * inverse, 0.0)
                    base_i = jnp.where(valid, 6.0 * (rhs_i * diag - 20.0 * imag * rhs_r) * inverse, 0.0)
                    base[2 * field, i, j] = base_r
                    base[2 * field + 1, i, j] = base_i
                    if not field:
                        coup[0, i, j] = couple_r
                        coup[1, i, j] = couple_i
                    cur[1, 2 * field, i + 1, j] = base_r + (couple_r * near_r[j] - couple_i * near_i[j])
                    cur[1, 2 * field + 1, i + 1, j] = base_i + (couple_r * near_i[j] + couple_i * near_r[j])
            return 0

        lax.fori_loop(0, count, first, 0)
        wrap_rows(1)

        def update(slot, i, store):
            for field in range(2):
                near_r = quarter_stencil(slot, 2 * field, i)
                near_i = quarter_stencil(slot, 2 * field + 1, i)
                for j in range(cols):
                    couple_r, couple_i = coup[0, i, j], coup[1, i, j]
                    base_r, base_i = base[2 * field, i, j], base[2 * field + 1, i, j]
                    cross_r, cross_i = couple_i * near_i[j], couple_i * near_r[j]
                    if field:
                        store(2, i, j, base_r + couple_r * near_r[j] + cross_r)
                        store(3, i, j, base_i + couple_r * near_i[j] - cross_i)
                    else:
                        store(0, i, j, base_r + couple_r * near_r[j] - cross_r)
                        store(1, i, j, base_i + couple_r * near_i[j] + cross_i)

        def sweep(s, _):
            slot = s % 2

            def store(c, i, j, value):
                cur[1 - slot, c, i + 1, j] = value

            def body(i, _):
                update(slot, i, store)
                return 0

            lax.fori_loop(0, count, body, 0)
            wrap_rows(1 - slot)
            return 0

        lax.fori_loop(1, SWEEPS - 1, sweep, 0)

        def store_last(c, i, j, value):
            nat[d + 1, c, j, strided(i), :] = value

        def last(i, _):
            update((SWEEPS - 1) % 2, i, store_last)
            return 0

        lax.fori_loop(0, count, last, 0)

        @pl.when(d + 1 < STEPS)
        def _():
            send_halos(d + 1)

        for k in range(1, group):
            field_copy(d, k, member).start()
        top = pl.multiple_of(HALO + member * chunk, 8)

        def keep(c, _):
            recv[d, member, c] = nat[d + 1, c, :, pl.ds(top, chunk), :]
            return 0

        lax.fori_loop(0, 4, keep, 0)

    def shifted(blocks, move):
        if move == 0:
            return blocks
        if move > 0:
            rolled = [pltpu.roll(b, LANES - move, 1) for b in blocks] + [zero]
            inside = lane < LANES - move
            return [jnp.where(inside, rolled[j], rolled[j + 1]) for j in range(cols)]
        rolled = [zero] + [pltpu.roll(b, -move, 1) for b in blocks]
        inside = lane >= -move
        return [jnp.where(inside, rolled[j + 1], rolled[j]) for j in range(cols)]

    def image_step(d):
        for k in range(1, group):
            field_copy(d, k, (member + k) % group).wait_recv()

        def block(rb, _):
            top = pl.multiple_of(rb * 8, 8)
            for o in range(OFFS):
                h = o - OFFS // 2

                def add(q, acc):
                    real = shifted([recv[d, q, 2, j, pl.ds(top, 8), :] for j in range(cols)], 2 * h)
                    imag = shifted([recv[d, q, 3, j, pl.ds(top, 8), :] for j in range(cols)], 2 * h)
                    return tuple(
                        acc[j]
                        + (recv[d, q, 0, j, pl.ds(top, 8), :] * real[j] + recv[d, q, 1, j, pl.ds(top, 8), :] * imag[j])
                        for j in range(cols)
                    )

                total = shifted(list(lax.fori_loop(0, group, add, (zero,) * cols)), -h)
                for j in range(cols):
                    img[d, o, pl.ds(top, 8), pl.ds(j * LANES, LANES)] = total[j] * (1.0 / math.sqrt(n))
            return 0

        lax.fori_loop(0, chunk // 8, block, 0)
        for k in range(1, n):
            image_copy(d, k, me).start()
        place = pl.multiple_of(member * chunk, 8)
        for o in range(per_dev):
            part[d, my_group, o, pl.ds(place, chunk), :] = img[d, me * per_dev + o]

    def pipeline(d, _):
        @pl.when(d < STEPS)
        def _():
            depth_step(d)

        @pl.when(d > 0)
        def _():
            image_step(d - 1)

        return 0

    lax.fori_loop(0, STEPS + 1, pipeline, 0)

    def finish(d, _):
        for k in range(1, n):
            image_copy(d, k, (me + k) % n).wait_recv()

        def merge(b, _):
            top = pl.multiple_of(b * 8, 8)
            for o in range(per_dev):
                total = part[d, 0, o, pl.ds(top, 8), :]
                for gr in range(1, groups):
                    total = total + part[d, gr, o, pl.ds(top, 8), :]
                out_ref[d, o, pl.ds(top, 8), :] = total
            return 0

        lax.fori_loop(0, rows // 8, merge, 0)
        for k in range(1, group):
            field_copy(d, k, member).wait_send()
        for k in range(1, n):
            image_copy(d, k, me).wait_send()

        @pl.when(has_up)
        def _():
            halo_copy(d, 0).wait_send()

        @pl.when(has_down)
        def _():
            halo_copy(d, 1).wait_send()

        return 0

    lax.fori_loop(0, STEPS, finish, 0)

    @pl.when(has_up)
    def _():
        vel_copy(0).wait_send()

    @pl.when(has_down)
    def _():
        vel_copy(1).wait_send()


def on_device(n, tiles, wave, velocity):
    rows, width = velocity.shape[1:]
    cols = width // LANES
    ext = rows + 2 * HALO
    count = ext // 8
    group = min(4, n)
    chunk = rows // group
    per_dev = OFFS // n
    f32 = jnp.float32
    dma = pltpu.SemaphoreType.DMA
    return pl.pallas_call(
        functools.partial(kernel, n, tiles, group),
        out_shape=jax.ShapeDtypeStruct((STEPS, per_dev, rows, width), f32),
        in_specs=[pl.BlockSpec(memory_space=pltpu.VMEM)] * 2,
        out_specs=pl.BlockSpec(memory_space=pltpu.VMEM),
        scratch_shapes=[
            pltpu.VMEM((STEPS + 1, 4, cols, ext, LANES), f32),
            pltpu.VMEM((STEPS, 2, 4, cols, HALO, LANES), f32),
            pltpu.VMEM((STEPS, cols, ext, LANES), f32),
            pltpu.VMEM((2, 4, count + 2, cols, 8, LANES), f32),
            pltpu.VMEM((4, count, cols, 8, LANES), f32),
            pltpu.VMEM((2, count, cols, 8, LANES), f32),
            pltpu.VMEM((STEPS, group, 4, cols, chunk, LANES), f32),
            pltpu.VMEM((STEPS, OFFS, chunk, width), f32),
            pltpu.VMEM((STEPS, n // group, per_dev, rows, width), f32),
            dma((2, 2)),
            dma((2, STEPS, 2)),
            dma((STEPS, group)),
            dma((STEPS, group)),
            dma((STEPS, n)),
            dma((STEPS, n)),
        ],
        compiler_params=pltpu.CompilerParams(
            collective_id=0, has_side_effects=True, vmem_limit_bytes=56 * 2**20
        ),
        name="migrate",
    )(wave, velocity)


def solution(mesh):
    placed = (P(None, None, "freq", "tile", None), P(None, "tile", None))
    return jax.shard_map(
        functools.partial(on_device, mesh.shape["freq"], mesh.shape["tile"]),
        mesh=mesh,
        in_specs=placed,
        out_specs=P(None, "freq", "tile", None),
        check_vma=False,
    )
```

time: 588 us -> 151 us (0.26)
  the two profiles are of different devices: /device:TPU:0 before, /device:TPU:31 now
where the time goes in v1:
time: 151 us
  Pallas kernels  148 us (98%)
  local copies, waits for them, and re-layouts  2.73 us (2%)
    pallas_call x1, Pallas kernels, on_device(): pl.pallas_call(functools.partial(kernel, n, tiles, group), out_shape=jax....  148 us

profile of v1, /device:TPU:31, one launch (start us, length us, event | category | flops | bytes accessed | tf_op | source)
XLA Modules:
  0.0 151.1 jit_solution(5387192729150150)
XLA Ops:
  0.0 148.3 %migrate.1 = f32[3,2,64,1024]{3,2,1,0:T(8,128)} custom-call(f32[2,2,1,64,1024]{4,3,2,1,0:T(8,128)} %wave_ref.1, f32[3,64,1024]{2,1,0:T(8,128)} %velocity_ref.1), custom_call_target="tpu_custom_call" | custom-call | tf_op jit(solution)/shard_map/migrate/pallas_call | solution.py:413
  148.3 2.7 %copy.4 = f32[3,2,64,1024]{3,2,1,0:T(8,128)} copy(f32[3,2,64,1024]{3,2,1,0:T(8,128)} %migrate.1) | data formatting | bytes 3145728

commit v2 on v1

--- a/solution.py
+++ b/solution.py
@@ -13,6 +13,7 @@
 OFFS = 16
 HALO = 8
 LANES = 128
+BATCH = 2
 
 pade_first = 0.376393
 pade_second = 0.478242
@@ -38,7 +39,7 @@
 
 
 def kernel(
-    n, tiles, group, wave_ref, velocity_ref, out_ref, nat, halo, vel, cur, base, coup, recv, img, part,
+    n, tiles, group, wave_ref, velocity_ref, out_ref, nat, halo, vel, cur_a, cur_b, base, coup, recv, img, part,
     vel_sems, halo_sems, field_send, field_recv, image_send, image_recv,
 ):
     rows, width = velocity_ref.shape[1:]
@@ -180,17 +181,17 @@
     def _():
         vel_copy(0).wait_recv()
 
-    def wrap_rows(slot):
+    def wrap_rows(ref):
         for c in range(4):
             for j in range(cols):
-                cur[slot, c, 0, j] = pltpu.roll(cur[slot, c, count, j], 1, 0)
-                cur[slot, c, count + 1, j] = pltpu.roll(cur[slot, c, 1, j], 7, 0)
-
-    def quarter_stencil(slot, c, i):
+                ref[c, 0, j] = pltpu.roll(ref[c, count, j], 1, 0)
+                ref[c, count + 1, j] = pltpu.roll(ref[c, 1, j], 7, 0)
+
+    def quarter_stencil(above, here, below):
         sums, to_right, to_left = [], [], []
         for j in range(cols):
-            pair = cur[slot, c, i, j] + cur[slot, c, i + 2, j]
-            mixed = cur[slot, c, i + 1, j] + 0.25 * pair
+            pair = above[j] + below[j]
+            mixed = here[j] + 0.25 * pair
             sums.append(pair)
             to_right.append(pltpu.roll(mixed, 1, 1))
             to_left.append(pltpu.roll(mixed, LANES - 1, 1))
@@ -201,6 +202,9 @@
             out.append(sums[j] + (left + right))
         return out
 
+    def rows_of(ref, c, i, many):
+        return [[ref[c, i + k, j] for j in range(cols)] for k in range(many + 2)]
+
     def depth_step(d):
         take_halos(d)
 
@@ -209,88 +213,100 @@
             for j in range(cols):
                 cosine, sine = cos_sin(angular * layer_thickness / vel[d, j, strided(i), :])
                 sr, si, rr, ri = [nat[d, c, j, strided(i), :] for c in range(4)]
-                cur[0, 0, i + 1, j] = jnp.where(valid, sr * cosine + si * sine, 0.0)
-                cur[0, 1, i + 1, j] = jnp.where(valid, si * cosine - sr * sine, 0.0)
-                cur[0, 2, i + 1, j] = jnp.where(valid, rr * cosine - ri * sine, 0.0)
-                cur[0, 3, i + 1, j] = jnp.where(valid, ri * cosine + rr * sine, 0.0)
+                cur_a[0, i + 1, j] = jnp.where(valid, sr * cosine + si * sine, 0.0)
+                cur_a[1, i + 1, j] = jnp.where(valid, si * cosine - sr * sine, 0.0)
+                cur_a[2, i + 1, j] = jnp.where(valid, rr * cosine - ri * sine, 0.0)
+                cur_a[3, i + 1, j] = jnp.where(valid, ri * cosine + rr * sine, 0.0)
             return 0
 
-        lax.fori_loop(0, count, screen, 0)
-        wrap_rows(0)
+        lax.fori_loop(0, count, screen, 0, unroll=2)
+        wrap_rows(cur_a)
 
         def first(i, _):
             valid = row_valid(i)
+            coefs = []
+            for j in range(cols):
+                speed = vel[d, j, strided(i), :]
+                real = pade_second * (speed / (angular * grid_spacing)) ** 2
+                imag = -pade_first * layer_thickness * speed / (2.0 * angular * grid_spacing**2)
+                diag = 6.0 + 20.0 * real
+                inverse = 1.0 / (diag * diag + 400.0 * imag * imag)
+                couple_r = jnp.where(valid, 4.0 * (real * diag + 20.0 * imag * imag) * inverse, 0.0)
+                couple_i = jnp.where(valid, 24.0 * imag * inverse, 0.0)
+                coup[0, i, j] = couple_r
+                coup[1, i, j] = couple_i
+                six = jnp.where(valid, 6.0 * inverse, 0.0)
+                coefs.append((real, imag, six * diag, 20.0 * six * imag, couple_r, couple_i))
             for field in range(2):
-                near_r = quarter_stencil(0, 2 * field, i)
-                near_i = quarter_stencil(0, 2 * field + 1, i)
+                r, m = 2 * field, 2 * field + 1
+                near_r = quarter_stencil(*rows_of(cur_a, r, i, 1))
+                near_i = quarter_stencil(*rows_of(cur_a, m, i, 1))
                 for j in range(cols):
-                    speed = vel[d, j, strided(i), :]
-                    real = pade_second * (speed / (angular * grid_spacing)) ** 2
-                    imag = -pade_first * layer_thickness * speed / (2.0 * angular * grid_spacing**2)
+                    real, imag, over_r, over_i, couple_r, couple_i = coefs[j]
                     if field:
-                        imag = -imag
-                    diag = 6.0 + 20.0 * real
-                    inverse = 1.0 / (diag * diag + 400.0 * imag * imag)
-                    couple_r = jnp.where(valid, 4.0 * (real * diag + 20.0 * imag * imag) * inverse, 0.0)
-                    couple_i = jnp.where(valid, 24.0 * imag * inverse, 0.0)
-                    u_r, u_i = cur[0, 2 * field, i + 1, j], cur[0, 2 * field + 1, i + 1, j]
-                    lap_r = (4.0 * near_r[j] - 20.0 * u_r) * (1.0 / 6.0)
-                    lap_i = (4.0 * near_i[j] - 20.0 * u_i) * (1.0 / 6.0)
+                        imag, over_i, couple_i = -imag, -over_i, -couple_i
+                    u_r, u_i = cur_a[r, i + 1, j], cur_a[m, i + 1, j]
+                    lap_r = (4.0 / 6.0) * near_r[j] - (20.0 / 6.0) * u_r
+                    lap_i = (4.0 / 6.0) * near_i[j] - (20.0 / 6.0) * u_i
                     rhs_r = u_r - (real * lap_r + imag * lap_i)
                     rhs_i = u_i - (real * lap_i - imag * lap_r)
-                    base_r = jnp.where(valid, 6.0 * (rhs_r * diag + 20.0 * imag * rhs_i) * inverse, 0.0)
-                    base_i = jnp.where(valid, 6.0 * (rhs_i * diag - 20.0 * imag * rhs_r) * inverse, 0.0)
-                    base[2 * field, i, j] = base_r
-                    base[2 * field + 1, i, j] = base_i
-                    if not field:
-                        coup[0, i, j] = couple_r
-                        coup[1, i, j] = couple_i
-                    cur[1, 2 * field, i + 1, j] = base_r + (couple_r * near_r[j] - couple_i * near_i[j])
-                    cur[1, 2 * field + 1, i + 1, j] = base_i + (couple_r * near_i[j] + couple_i * near_r[j])
+                    base_r = rhs_r * over_r + over_i * rhs_i
+                    base_i = rhs_i * over_r - over_i * rhs_r
+                    base_r = jnp.where(valid, base_r, 0.0)
+                    base_i = jnp.where(valid, base_i, 0.0)
+                    base[r, i, j] = base_r
+                    base[m, i, j] = base_i
+                    cur_b[r, i + 1, j] = base_r + (couple_r * near_r[j] - couple_i * near_i[j])
+                    cur_b[m, i + 1, j] = base_i + (couple_r * near_i[j] + couple_i * near_r[j])
             return 0
 
         lax.fori_loop(0, count, first, 0)
-        wrap_rows(1)
-
-        def update(slot, i, store):
+        wrap_rows(cur_b)
+
+        def update(ref, i, many, store):
             for field in range(2):
-                near_r = quarter_stencil(slot, 2 * field, i)
-                near_i = quarter_stencil(slot, 2 * field + 1, i)
-                for j in range(cols):
-                    couple_r, couple_i = coup[0, i, j], coup[1, i, j]
-                    base_r, base_i = base[2 * field, i, j], base[2 * field + 1, i, j]
-                    cross_r, cross_i = couple_i * near_i[j], couple_i * near_r[j]
-                    if field:
-                        store(2, i, j, base_r + couple_r * near_r[j] + cross_r)
-                        store(3, i, j, base_i + couple_r * near_i[j] - cross_i)
-                    else:
-                        store(0, i, j, base_r + couple_r * near_r[j] - cross_r)
-                        store(1, i, j, base_i + couple_r * near_i[j] + cross_i)
-
-        def sweep(s, _):
-            slot = s % 2
-
-            def store(c, i, j, value):
-                cur[1 - slot, c, i + 1, j] = value
-
-            def body(i, _):
-                update(slot, i, store)
+                r, m = 2 * field, 2 * field + 1
+                lines_r, lines_i = rows_of(ref, r, i, many), rows_of(ref, m, i, many)
+                for k in range(many):
+                    near_r = quarter_stencil(*lines_r[k : k + 3])
+                    near_i = quarter_stencil(*lines_i[k : k + 3])
+                    for j in range(cols):
+                        couple_r, couple_i = coup[0, i + k, j], coup[1, i + k, j]
+                        cross_r, cross_i = couple_i * near_i[j], couple_i * near_r[j]
+                        main_r = base[r, i + k, j] + couple_r * near_r[j]
+                        main_i = base[m, i + k, j] + couple_r * near_i[j]
+                        if field:
+                            store(r, i + k, j, main_r + cross_r)
+                            store(m, i + k, j, main_i - cross_i)
+                        else:
+                            store(r, i + k, j, main_r - cross_r)
+                            store(m, i + k, j, main_i + cross_i)
+
+        def over_rows(ref, store):
+            def body(b, _):
+                update(ref, b * BATCH, BATCH, store)
                 return 0
 
-            lax.fori_loop(0, count, body, 0)
-            wrap_rows(1 - slot)
-            return 0
-
-        lax.fori_loop(1, SWEEPS - 1, sweep, 0)
+            lax.fori_loop(0, count // BATCH, body, 0)
+
+        def store_a(c, i, j, value):
+            cur_a[c, i + 1, j] = value
+
+        def store_b(c, i, j, value):
+            cur_b[c, i + 1, j] = value
 
         def store_last(c, i, j, value):
             nat[d + 1, c, j, strided(i), :] = value
 
-        def last(i, _):
-            update((SWEEPS - 1) % 2, i, store_last)
-            return 0
-
-        lax.fori_loop(0, count, last, 0)
+        def two_sweeps(_, carry):
+            over_rows(cur_b, store_a)
+            wrap_rows(cur_a)
+            over_rows(cur_a, store_b)
+            wrap_rows(cur_b)
+            return carry
+
+        lax.fori_loop(0, (SWEEPS - 2) // 2, two_sweeps, 0)
+        over_rows(cur_b, store_last)
 
         @pl.when(d + 1 < STEPS)
         def _():
@@ -326,16 +342,14 @@
             for o in range(OFFS):
                 h = o - OFFS // 2
 
-                def add(q, acc):
+                total = [None] * cols
+                for q in range(group):
                     real = shifted([recv[d, q, 2, j, pl.ds(top, 8), :] for j in range(cols)], 2 * h)
                     imag = shifted([recv[d, q, 3, j, pl.ds(top, 8), :] for j in range(cols)], 2 * h)
-                    return tuple(
-                        acc[j]
-                        + (recv[d, q, 0, j, pl.ds(top, 8), :] * real[j] + recv[d, q, 1, j, pl.ds(top, 8), :] * imag[j])
-                        for j in range(cols)
-                    )
-
-                total = shifted(list(lax.fori_loop(0, group, add, (zero,) * cols)), -h)
+                    for j in range(cols):
+                        term = recv[d, q, 0, j, pl.ds(top, 8), :] * real[j] + recv[d, q, 1, j, pl.ds(top, 8), :] * imag[j]
+                        total[j] = term if q == 0 else total[j] + term
+                total = shifted(total, -h)
                 for j in range(cols):
                     img[d, o, pl.ds(top, 8), pl.ds(j * LANES, LANES)] = total[j] * (1.0 / math.sqrt(n))
             return 0
@@ -419,7 +433,8 @@
             pltpu.VMEM((STEPS + 1, 4, cols, ext, LANES), f32),
             pltpu.VMEM((STEPS, 2, 4, cols, HALO, LANES), f32),
             pltpu.VMEM((STEPS, cols, ext, LANES), f32),
-            pltpu.VMEM((2, 4, count + 2, cols, 8, LANES), f32),
+            pltpu.VMEM((4, count + 2, cols, 8, LANES), f32),
+            pltpu.VMEM((4, count + 2, cols, 8, LANES), f32),
             pltpu.VMEM((4, count, cols, 8, LANES), f32),
             pltpu.VMEM((2, count, cols, 8, LANES), f32),
             pltpu.VMEM((STEPS, group, 4, cols, chunk, LANES), f32),

time: 151 us -> 126 us (0.83)
  Pallas kernels: 148 us -> 123 us
    pallas_call x1, Pallas kernels: 148 us -> 123 us  [on_device(): pl.pallas_call(functools.partial(kernel, n, tiles, group), out_shape=jax....]
where the time goes in v2:
time: 126 us
  Pallas kernels  123 us (98%)
  local copies, waits for them, and re-layouts  2.73 us (2%)
    pallas_call x1, Pallas kernels, on_device(): pl.pallas_call(functools.partial(kernel, n, tiles, group), out_shape=jax....  123 us
    unnamed x1, local copies, waits for them, and re-layouts  2.73 us

profile of v2, /device:TPU:31, one launch (start us, length us, event | category | flops | bytes accessed | tf_op | source)
XLA Modules:
  0.0 126.2 jit_solution(10793901002697212884)
XLA Ops:
  0.0 123.4 %migrate.1 = f32[3,2,64,1024]{3,2,1,0:T(8,128)} custom-call(f32[2,2,1,64,1024]{4,3,2,1,0:T(8,128)} %wave_ref.1, f32[3,64,1024]{2,1,0:T(8,128)} %velocity_ref.1), custom_call_target="tpu_custom_call" | custom-call | tf_op jit(solution)/shard_map/migrate/pallas_call | solution.py:427
  123.5 2.7 %copy.4 = f32[3,2,64,1024]{3,2,1,0:T(8,128)} copy(f32[3,2,64,1024]{3,2,1,0:T(8,128)} %migrate.1) | data formatting | bytes 3145728

commit v3 on v2

--- a/solution.py
+++ b/solution.py
@@ -306,6 +306,11 @@
             return carry
 
         lax.fori_loop(0, (SWEEPS - 2) // 2, two_sweeps, 0)
+
+        @pl.when(d == 1)
+        def _():
+            image_step(0)
+
         over_rows(cur_b, store_last)
 
         @pl.when(d + 1 < STEPS)
@@ -366,7 +371,7 @@
         def _():
             depth_step(d)
 
-        @pl.when(d > 0)
+        @pl.when(d > 1)
         def _():
             image_step(d - 1)
 

time: 126 us -> 128 us (1.016)
  Pallas kernels: 123 us -> 125 us
    pallas_call x1, Pallas kernels: 123 us -> 125 us  [on_device(): pl.pallas_call(functools.partial(kernel, n, tiles, group), out_shape=jax....]
where the time goes in v3:
time: 128 us
  Pallas kernels  125 us (98%)
  local copies, waits for them, and re-layouts  2.73 us (2%)
    pallas_call x1, Pallas kernels, on_device(): pl.pallas_call(functools.partial(kernel, n, tiles, group), out_shape=jax....  125 us
    unnamed x1, local copies, waits for them, and re-layouts  2.73 us

profile of v3, /device:TPU:31, one launch (start us, length us, event | category | flops | bytes accessed | tf_op | source)
XLA Modules:
  0.0 127.7 jit_solution(7987493606260042880)
XLA Ops:
  0.0 125.0 %migrate.1 = f32[3,2,64,1024]{3,2,1,0:T(8,128)} custom-call(f32[2,2,1,64,1024]{4,3,2,1,0:T(8,128)} %wave_ref.1, f32[3,64,1024]{2,1,0:T(8,128)} %velocity_ref.1), custom_call_target="tpu_custom_call" | custom-call | tf_op jit(solution)/shard_map/migrate/pallas_call | solution.py:432
  125.0 2.7 %copy.4 = f32[3,2,64,1024]{3,2,1,0:T(8,128)} copy(f32[3,2,64,1024]{3,2,1,0:T(8,128)} %migrate.1) | data formatting | bytes 3145728
